TPU v7x, 512 devices: a whole 4x8x8 slice. The times are simulated.
512 devices in a mesh: fsdp: 64 (over y, x, core), cent: 8 (over z).
Axes of the slice: x: 4, y: 8, z: 8, core: 2. Of those that a mesh axis runs over, the one named last changes fastest.
Arguments:
- attention: bfloat16 [8192, 4096], P('fsdp', 'cent'), may hold values from -6 to 6
- w_out: bfloat16 [4096, 4096], P('cent', 'fsdp'), may hold values from -0.09375 to 0.09375
- hidden: bfloat16 [8192, 4096], P(('fsdp', 'cent')), may hold values from -6 to 6
- norm_gain: bfloat16 [4096], replicated, may hold values from 0.099609375 to 1.8984375
- centroids: bfloat16 [512, 4096], P('cent'), may hold values from -3 to 3
- token_codes: int32 [8192], P(('fsdp', 'cent')), may hold values from 0 to 63, as said below
- tile_lists: int32 [64, 8], P('fsdp'), may hold values from 0 to 63, as said below
Outputs:
- centroid_sums: float32 [512, 4096], P('cent', 'fsdp')
- residual_gram: float32 [4096, 4096], P('fsdp', 'cent')
Inputs may be any that keep to these rules, and one draw needn't show every extreme that they name: `token_codes`: token t belongs to block t // 128; its code k names centroid k % 8 of the tile at slot k // 8 of that block's list; every slot of a block's list is used. `tile_lists`: each row holds 8 distinct tile ids in ascending order; tile j holds centroids j * 8 to j * 8 + 7, and centroid g belongs to owner shard g // 64; in every row at most 2 listed tiles share an owner, and exactly 2 do for some owner.
All inputs are finite; a program needn't handle non-finite values.
Results may differ from a plain program's by a relative error of at most 0.0085.
Values may be sent and summed in bfloat16 or wider, within the bound.
A program may use at most 64 MiB of HBM per device.

v0:
```python
import jax
import jax.numpy as jnp
from jax import lax
from jax.sharding import PartitionSpec as P

TILE = 8
LT = 8


def shards(attention, w_out, hidden, norm_gain, centroids, token_codes, tile_lists):
    tok_dev = hidden.shape[0]
    feat_dim = hidden.shape[1]
    n_fsdp = lax.axis_size("fsdp")
    n_cent = lax.axis_size("cent")
    cap_slots = max(2, 2 * LT // n_cent)
    partial_out = jnp.dot(
        attention,
        lax.all_gather(w_out, "fsdp", axis=1, tiled=True),
        preferred_element_type=jnp.float32,
    )
    head_sum = lax.psum_scatter(
        partial_out.astype(jnp.bfloat16), "cent", scatter_dimension=0, tiled=True
    ).astype(jnp.float32)
    mixed_rows = hidden.astype(jnp.float32) + head_sum
    normed = (
        mixed_rows
        * lax.rsqrt(jnp.mean(mixed_rows * mixed_rows, axis=1, keepdims=True) + 1e-05)
        * norm_gain.astype(jnp.float32)
    )
    cent_dev = centroids.shape[0]
    own_tiles = cent_dev // TILE
    owner_idx = lax.axis_index("cent")
    listed = tile_lists[0]
    local_tile = listed - owner_idx * own_tiles
    owned_here = (local_tile >= 0) & (local_tile < own_tiles)
    safe_tile = jnp.clip(local_tile, 0, own_tiles - 1)
    tiles_here = centroids.reshape(own_tiles, TILE, feat_dim)
    slot_of = token_codes // TILE
    offset = token_codes % TILE
    rank_mine = jnp.cumsum(owned_here.astype(jnp.int32)) - 1
    chosen = owned_here[None, :] & (
        rank_mine[None, :] == jnp.arange(cap_slots, dtype=jnp.int32)[:, None]
    )
    send_tile = jnp.sum(jnp.where(chosen, safe_tile[None, :], 0), axis=1)
    filled = jnp.any(chosen, axis=1)
    outgoing = jnp.where(
        filled[:, None, None],
        jnp.take(tiles_here, send_tile, axis=0),
        jnp.zeros((cap_slots, TILE, feat_dim), jnp.bfloat16),
    )
    arrived = lax.all_gather(outgoing, "cent", axis=0, tiled=True)
    owner_of = listed // own_tiles
    list_pos = jnp.arange(LT, dtype=jnp.int32)
    earlier = (owner_of[None, :] == owner_of[:, None]) & (list_pos[None, :] < list_pos[:, None])
    rank_all = jnp.sum(earlier.astype(jnp.int32), axis=1)
    where_tile = owner_of * cap_slots + rank_all
    tile_rows = arrived.reshape(-1, feat_dim)
    centers = jnp.take(tile_rows, where_tile[slot_of] * TILE + offset, axis=0)
    residual = (normed - centers.astype(jnp.float32)).astype(jnp.bfloat16)
    onehot = (token_codes[None, :] == jnp.arange(LT * TILE, dtype=jnp.int32)[:, None]).astype(
        jnp.bfloat16
    )
    slot_part = jnp.dot(onehot, residual, preferred_element_type=jnp.float32)
    slot_sum = lax.psum(slot_part.astype(jnp.bfloat16), "cent").astype(jnp.float32)
    target = (local_tile[:, None] * TILE + jnp.arange(TILE, dtype=jnp.int32)[None, :]).reshape(-1)
    valid_rows = jnp.repeat(owned_here, TILE)
    placer = (
        (jnp.arange(cent_dev, dtype=jnp.int32)[:, None] == target[None, :]) & valid_rows[None, :]
    ).astype(jnp.float32)
    dense_part = jnp.dot(
        placer, slot_sum, precision=lax.Precision.HIGHEST, preferred_element_type=jnp.float32
    )
    centroid_sums = lax.psum_scatter(dense_part, "fsdp", scatter_dimension=1, tiled=True)
    rows_dev = feat_dim // n_fsdp
    row_start = lax.axis_index("fsdp") * rows_dev
    shard_rows = lax.all_gather(residual, "fsdp", axis=0, tiled=True)
    left_cols = lax.dynamic_slice_in_dim(shard_rows, row_start, rows_dev, 1)
    gram_part = lax.dot_general(
        left_cols, shard_rows, (((0,), (0,)), ((), ())), preferred_element_type=jnp.float32
    )
    gram_sum = lax.psum_scatter(gram_part, "cent", scatter_dimension=1, tiled=True)
    tokens_all = tok_dev * n_fsdp * n_cent
    return (centroid_sums, gram_sum / tokens_all)


def solution(mesh):
    in_specs = (
        P("fsdp", "cent"),
        P("cent", "fsdp"),
        P(("fsdp", "cent"), None),
        P(),
        P("cent", None),
        P(("fsdp", "cent")),
        P("fsdp", None),
    )
    out_specs = (P("cent", "fsdp"), P("fsdp", "cent"))
    return jax.shard_map(shards, mesh=mesh, in_specs=in_specs, out_specs=out_specs, check_vma=False)
```

profile of v0, /device:TPU:2, one launch (start us, length us, event | category | flops | bytes accessed | tf_op | source)
XLA Modules:
  0.0 561.0 jit_solution(6380447563696765636)
XLA Ops:
  7.2 0.0 copy-start
  7.2 0.0 copy-start.4
  7.2 0.0 copy-start.3
  7.2 0.0 all-gather.4.cloned.1.call-start
  7.3 0.7 all-gather.4.cloned.1.call-update
  7.9 0.0 all-gather.6.cloned.1.call-start
  8.0 0.7 convert_bitcast_fusion
  8.7 0.2 reduce-window.8
  8.9 0.7 fusion.11
  9.5 0.1 select_reduce_fusion
  9.7 0.0 copy-done
  9.7 0.6 gather_fusion.1
  10.2 0.1 fusion.8
  10.4 0.7 select_select_fusion
  11.1 0.0 all-gather.6.cloned.1.call-update
  11.1 0.0 reduce-scatter.6.cloned.1.call-start
  11.2 88.0 %all-gather.4.cloned.1.call-done = bf16[512,4096]{0,1:T(8,128)(2,1)} async-done(((bf16[512,64]{0,1:T(8,128)(2,1)}), bf16[512,4096]{0,1:T(8,128)(2,1)}) %all-gather.4.cloned.1.call-update) | async-done | bytes 4194320 | tf_op jit(solution)/shard_map/all_gather | solution.py:18
  99.2 4.8 convolution_convert_fusion
  104.0 0.0 reduce-scatter.6.cloned.1.call-update
  104.0 0.0 all-reduce.2.cloned.1.call-start
  104.1 0.2 convert_reduce_fusion
  104.3 0.7 gather_fusion
  105.0 37.3 %all-gather.6.cloned.1.call-done = bf16[16,8,4096]{2,1,0:T(8,128)(2,1)} async-done(((bf16[2,8,4096]{2,1,0:T(8,128)(2,1)}), bf16[16,8,4096]{2,1,0:T(8,128)(2,1)}) %all-gather.6.cloned.1.call-update) | async-done | bytes 1048592 | tf_op jit(solution)/shard_map/all_gather | solution.py:51
  142.4 2.1 gather_fusion.2
  144.5 41.3 %reduce-scatter.6.cloned.1.call-done = bf16[16,4096]{1,0:T(8,128)(2,1)} async-done(((bf16[128,4096]{1,0:T(8,128)(2,1)}), bf16[16,4096]{1,0:T(8,128)(2,1)}) %reduce-scatter.6.cloned.1.call-update) | async-done | bytes 131088 | tf_op jit(solution)/shard_map/reduce_scatter | solution.py:21
  185.8 1.1 multiply_reduce_fusion
  186.9 1.0 subtract_convert_fusion
  187.9 0.0 copy-start.1
  187.9 1.1 convolution_convert_fusion.1
  189.1 0.0 all-reduce.2.cloned.1.call-update
  189.1 0.0 all-gather.8.cloned.1.call-start
  189.1 0.5 all-gather.8.cloned.1.call-update
  189.7 0.0 reduce-scatter.10.cloned.1.call-start
  189.7 0.1 iota_add_fusion
  189.8 0.1 add.94
  189.9 0.1 broadcast_in_dim.69
  190.0 0.1 and.75
  190.1 77.2 %all-reduce.2.cloned.1.call-done = bf16[64,4096]{1,0:T(8,128)(2,1)} async-done(((bf16[64,4096]{1,0:T(8,128)(2,1)}), bf16[64,4096]{1,0:T(8,128)(2,1)}) %all-reduce.2.cloned.1.call-update) | async-done | bytes 524304 | tf_op jit(solution)/shard_map/psum | solution.py:64
  267.3 2.9 convolution_bitcast_fusion
  270.2 0.0 reduce-scatter.10.cloned.1.call-update
  270.2 0.0 reduce-scatter.8.cloned.1.call-start
  270.3 85.8 %all-gather.8.cloned.1.call-done = bf16[1024,4096]{1,0:T(8,128)(2,1)} async-done(((bf16[16,4096]{1,0:T(8,128)(2,1)}), bf16[1024,4096]{1,0:T(8,128)(2,1)}) %all-gather.8.cloned.1.call-update) | async-done | bytes 8388624 | tf_op jit(solution)/shard_map/all_gather | solution.py:76
  356.1 6.1 %fusion = f32[64,4096]{1,0:T(8,128)} fusion(bf16[1024,4096]{1,0:T(8,128)(2,1)} %all-gather.8.cloned.1.call-done, s32[]{:T(128)S(6)} %select_n.78), kind=kOutput, calls=%fused_computation.6 | convolution fusion | flops 536870912 | bytes 9699332 | tf_op jit(solution)/shard_map/dot_general | solution.py:78
  362.3 0.0 reduce-scatter.8.cloned.1.call-update
  362.3 145.4 %reduce-scatter.10.cloned.1.call-done = f32[64,64]{1,0:T(8,128)} async-done(((f32[4096,64]{1,0:T(8,128)}), f32[64,64]{1,0:T(8,128)}) %reduce-scatter.10.cloned.1.call-update) | async-done | bytes 16400
  507.7 1.5 copy.10
  509.1 43.5 %reduce-scatter.8.cloned.1.call-done = f32[64,512]{1,0:T(8,128)} async-done(((f32[64,4096]{1,0:T(8,128)}), f32[64,512]{1,0:T(8,128)}) %reduce-scatter.8.cloned.1.call-update) | async-done | bytes 131088 | tf_op jit(solution)/shard_map/reduce_scatter | solution.py:81
  552.6 1.6 broadcast_multiply_fusion
  (20 shorter events, 0.1 us)
Async XLA Ops:
  7.2 2.5 copy-start
  7.2 96.9 %copy-start.4 = (s32[1,8]{1,0:T(1,128)S(1)}, s32[1,8]{1,0:T(1,128)}, u32[]{:S(2)}) copy-start(s32[1,8]{1,0:T(1,128)} %param.13) | copy-start | bytes 100
  7.2 96.9 %copy-start.3 = (bf16[4096]{0:T(1024)(128)(2,1)S(1)}, bf16[4096]{0:T(1024)(128)(2,1)}, u32[]{:S(2)}) copy-start(bf16[4096]{0:T(1024)(128)(2,1)} %param.10) | copy-start | bytes 24580
  7.2 96.9 %copy-start.5 = (s32[16]{0:T(128)S(1)}, s32[16]{0:T(128)}, u32[]{:S(2)}) copy-start(s32[16]{0:T(128)} %param.12) | copy-start | bytes 196
  7.2 92.0 %all-gather.4.cloned.1.call-start = ((), (), s32[]{:S(2)}) async-start(), calls=%async_computation.3 | async-start | bytes 4259840 | tf_op jit(solution)/shard_map/all_gather | solution.py:18
  7.9 134.4 %all-gather.6.cloned.1.call-start = ((), (), s32[]{:S(2)}) async-start(), calls=%async_computation.5 | async-start | bytes 1179648 | tf_op jit(solution)/shard_map/all_gather | solution.py:51
  11.1 174.7 %copy-start.2 = (bf16[16,4096]{1,0:T(8,128)(2,1)S(1)}, bf16[16,4096]{1,0:T(8,128)(2,1)}, u32[]{:S(2)}) copy-start(bf16[16,4096]{1,0:T(8,128)(2,1)} %param.9) | copy-start | bytes 393220
  11.1 174.7 %reduce-scatter.6.cloned.1.call-start = ((), (), s32[]{:S(2)}) async-start(), calls=%async_computation.4 | async-start | bytes 1179648 | tf_op jit(solution)/shard_map/reduce_scatter | solution.py:21
  104.0 163.3 %all-reduce.2.cloned.1.call-start = ((), (), s32[]{:S(2)}) async-start(), calls=%async_computation.6 | async-start | bytes 1048576 | tf_op jit(solution)/shard_map/psum | solution.py:64
  187.9 1.2 copy-start.1
  189.1 167.0 %all-gather.8.cloned.1.call-start = ((), (), s32[]{:S(2)}) async-start(), calls=%async_computation.7 | async-start | bytes 8519680 | tf_op jit(solution)/shard_map/all_gather | solution.py:76
  189.7 318.0 %reduce-scatter.10.cloned.1.call-start = ((), (), s32[]{:S(2)}) async-start(), calls=%async_computation.9 | async-start | bytes 2129920
  270.2 282.3 %reduce-scatter.8.cloned.1.call-start = ((), (), s32[]{:S(2)}) async-start(), calls=%async_computation.8 | async-start | bytes 1179648 | tf_op jit(solution)/shard_map/reduce_scatter | solution.py:81
Sparse Core Ops, SparseCore 0:
  11.4 87.8 all-gather.3
  101.9 40.4 all-gather.5
  145.2 40.5 reduce-scatter.5
  189.2 78.0 all-reduce.1
  271.1 84.9 all-gather.7
  360.6 147.0 reduce-scatter.9
  510.5 42.0 reduce-scatter.7
where the time goes:
time: 561 us
  waiting for transfers between devices  520 us (93%)
  matrix products  15 us (3%)
  between operations  14.3 us (3%)
  other arithmetic  6.51 us (1%)
    unnamed x8, waiting for transfers between devices  147 us
    all_gather x1, waiting for transfers between devices, shards(): lax.all_gather(w_out, 'fsdp', axis=1, tiled=True)  88 us
    all_gather x1, waiting for transfers between devices, shards(): shard_rows = lax.all_gather(residual, 'fsdp', axis=0, tiled=True)  85.8 us
    psum x1, waiting for transfers between devices, shards(): lax.psum(slot_part.astype(jnp.bfloat16), 'cent').astype(jnp.float32)  77.2 us
    reduce_scatter x1, waiting for transfers between devices, shards(): lax.psum_scatter(gram_part, 'cent', scatter_dimension=1, tiled=True)  43.5 us
    reduce_scatter x1, waiting for transfers between devices, shards(): lax.psum_scatter(partial_out.astype(jnp.bfloat16), 'cent', scatter_dimens...  41.3 us
    all_gather x1, waiting for transfers between devices, shards(): arrived = lax.all_gather(outgoing, 'cent', axis=0, tiled=True)  37.3 us
  transfers between devices with their start and end apart: 7, of which 7 were waited for; matrix products, arithmetic and copies ran while one was open for 4% of the time, Pallas kernels for 0%

commit v1 on v0

--- a/solution.py
+++ b/solution.py
@@ -5,6 +5,13 @@
 
 TILE = 8
 LT = 8
+
+
+def exchange_gather(block, name, d):
+    size = lax.axis_size(name)
+    tiles = jnp.stack([block for _ in range(size)])
+    tiles = lax.all_to_all(tiles, name, split_axis=0, concat_axis=0)
+    return jnp.concatenate(tiles, axis=d)
 
 
 def shards(attention, w_out, hidden, norm_gain, centroids, token_codes, tile_lists):
@@ -73,7 +80,7 @@
     centroid_sums = lax.psum_scatter(dense_part, "fsdp", scatter_dimension=1, tiled=True)
     rows_dev = feat_dim // n_fsdp
     row_start = lax.axis_index("fsdp") * rows_dev
-    shard_rows = lax.all_gather(residual, "fsdp", axis=0, tiled=True)
+    shard_rows = exchange_gather(residual, "fsdp", 0)
     left_cols = lax.dynamic_slice_in_dim(shard_rows, row_start, rows_dev, 1)
     gram_part = lax.dot_general(
         left_cols, shard_rows, (((0,), (0,)), ((), ())), preferred_element_type=jnp.float32

time: 561 us -> 494 us (0.88)
  the two profiles are of different devices: /device:TPU:2 before, /device:TPU:4 now
where the time goes in v1:
time: 494 us
  waiting for transfers between devices  438 us (89%)
  matrix products  15 us (3%)
  between operations  14.3 us (3%)
  starting transfers between devices  10.7 us (2%)
  local copies, waits for them, and re-layouts  9.32 us (2%)
  other arithmetic  6.51 us (1%)
    all_to_all x1, waiting for transfers between devices, exchange_gather(): tiles = lax.all_to_all(tiles, name, split_axis=0, concat_axis=0)  104 us
    all_gather x1, waiting for transfers between devices, shards(): lax.all_gather(w_out, 'fsdp', axis=1, tiled=True)  87.8 us
    psum x1, waiting for transfers between devices, shards(): lax.psum(slot_part.astype(jnp.bfloat16), 'cent').astype(jnp.float32)  79.6 us
    unnamed x7, waiting for transfers between devices  44.9 us
    reduce_scatter x1, waiting for transfers between devices, shards(): lax.psum_scatter(gram_part, 'cent', scatter_dimension=1, tiled=True)  43.3 us
    reduce_scatter x1, waiting for transfers between devices, shards(): lax.psum_scatter(partial_out.astype(jnp.bfloat16), 'cent', scatter_dimens...  41.3 us
    all_gather x1, waiting for transfers between devices, shards(): arrived = lax.all_gather(outgoing, 'cent', axis=0, tiled=True)  37.6 us
    all_to_all x1, starting transfers between devices, exchange_gather(): tiles = lax.all_to_all(tiles, name, split_axis=0, concat_axis=0)  10.5 us
  transfers between devices with their start and end apart: 7, of which 7 were waited for; matrix products, arithmetic and copies ran while one was open for 5% of the time, Pallas kernels for 0%

profile of v1, /device:TPU:4, one launch (start us, length us, event | category | flops | bytes accessed | tf_op | source)
XLA Modules:
  0.0 493.9 jit_solution(17795808136419230780)
XLA Ops:
  7.2 0.0 copy-start
  7.2 0.0 copy-start.3
  7.2 0.0 copy-start.2
  7.2 0.0 all-gather.3.cloned.1.call-start
  7.3 0.7 all-gather.3.cloned.1.call-update
  7.9 0.0 all-gather.5.cloned.1.call-start
  8.0 0.7 convert_bitcast_fusion
  8.7 0.2 reduce-window.8
  8.9 0.7 fusion.11
  9.5 0.1 select_reduce_fusion
  9.7 0.6 gather_fusion.1
  10.2 0.1 fusion.8
  10.4 0.7 select_select_fusion
  11.1 0.0 all-gather.5.cloned.1.call-update
  11.1 0.0 reduce-scatter.6.cloned.1.call-start
  11.2 87.8 %all-gather.3.cloned.1.call-done = bf16[512,4096]{0,1:T(8,128)(2,1)} async-done(((bf16[512,64]{0,1:T(8,128)(2,1)}), bf16[512,4096]{0,1:T(8,128)(2,1)}) %all-gather.3.cloned.1.call-update) | async-done | bytes 4194320 | tf_op jit(solution)/shard_map/all_gather | solution.py:25
  99.0 4.7 convolution_convert_fusion
  103.7 0.0 reduce-scatter.6.cloned.1.call-update
  103.7 0.0 copy-done.2
  103.8 0.0 copy-done.4
  103.8 0.2 convert_reduce_fusion
  104.0 0.7 gather_fusion
  104.7 37.6 %all-gather.5.cloned.1.call-done = bf16[16,8,4096]{2,1,0:T(8,128)(2,1)} async-done(((bf16[2,8,4096]{2,1,0:T(8,128)(2,1)}), bf16[16,8,4096]{2,1,0:T(8,128)(2,1)}) %all-gather.5.cloned.1.call-update) | async-done | bytes 1048592 | tf_op jit(solution)/shard_map/all_gather | solution.py:58
  142.4 2.1 gather_fusion.2
  144.5 41.3 %reduce-scatter.6.cloned.1.call-done = bf16[16,4096]{1,0:T(8,128)(2,1)} async-done(((bf16[128,4096]{1,0:T(8,128)(2,1)}), bf16[16,4096]{1,0:T(8,128)(2,1)}) %reduce-scatter.6.cloned.1.call-update) | async-done | bytes 131088 | tf_op jit(solution)/shard_map/reduce_scatter | solution.py:28
  185.8 1.1 multiply_reduce_fusion
  186.9 1.0 subtract_convert_fusion
  187.9 4.3 stack.2
  192.2 10.5 %all-to-all-start = ((bf16[64,16,4096]{2,1,0:T(8,128)(2,1)}), bf16[64,16,4096]{2,1,0:T(8,128)(2,1)}, u32[]{:S(2)}, u32[]{:S(2)}) async-start(bf16[64,16,4096]{2,1,0:T(8,128)(2,1)} %stack.2), calls=%async_computation.1 | async-start | bytes 16777216 | tf_op jit(solution)/shard_map/all_to_all | solution.py:13
  202.6 0.0 all-reduce.2.cloned.1.call-start
  202.7 1.1 convolution_convert_fusion.1
  203.8 0.0 all-reduce.2.cloned.1.call-update
  203.8 0.0 reduce-scatter.10.cloned.1.call-start
  203.8 0.1 broadcast_in_dim.69
  203.9 0.1 and.75
  204.0 0.1 iota_add_fusion
  204.1 0.1 add.94
  204.2 79.6 %all-reduce.2.cloned.1.call-done = bf16[64,4096]{1,0:T(8,128)(2,1)} async-done(((bf16[64,4096]{1,0:T(8,128)(2,1)}), bf16[64,4096]{1,0:T(8,128)(2,1)}) %all-reduce.2.cloned.1.call-update) | async-done | bytes 524304 | tf_op jit(solution)/shard_map/psum | solution.py:71
  283.7 2.9 convolution_bitcast_fusion
  286.6 0.0 reduce-scatter.10.cloned.1.call-update
  286.7 0.0 reduce-scatter.8.cloned.1.call-start
  286.7 103.6 %all-to-all-done = bf16[64,16,4096]{2,1,0:T(8,128)(2,1)} async-done(((bf16[64,16,4096]{2,1,0:T(8,128)(2,1)}), bf16[64,16,4096]{2,1,0:T(8,128)(2,1)}, u32[]{:S(2)}, u32[]{:S(2)}) %all-to-all-start) | async-done | bytes 8388640 | tf_op jit(solution)/shard_map/all_to_all | solution.py:13
  390.3 6.3 %fusion = f32[64,4096]{1,0:T(8,128)} fusion(bf16[1024,4096]{1,0:T(8,128)(2,1)} %bitcast.10, s32[]{:T(128)S(6)} %select_n.78), kind=kOutput, calls=%fused_computation.6 | convolution fusion | flops 536870912 | bytes 9699332 | tf_op jit(solution)/shard_map/dot_general | solution.py:85
  396.6 0.0 reduce-scatter.8.cloned.1.call-update
  396.6 44.1 %reduce-scatter.10.cloned.1.call-done = f32[64,64]{1,0:T(8,128)} async-done(((f32[4096,64]{1,0:T(8,128)}), f32[64,64]{1,0:T(8,128)}) %reduce-scatter.10.cloned.1.call-update) | async-done | bytes 16400
  440.7 1.5 copy.10
  442.1 43.3 %reduce-scatter.8.cloned.1.call-done = f32[64,512]{1,0:T(8,128)} async-done(((f32[64,4096]{1,0:T(8,128)}), f32[64,512]{1,0:T(8,128)}) %reduce-scatter.8.cloned.1.call-update) | async-done | bytes 131088 | tf_op jit(solution)/shard_map/reduce_scatter | solution.py:88
  485.5 1.6 broadcast_multiply_fusion
  (18 shorter events, 0.1 us)
Async XLA Ops:
  7.2 2.5 copy-start
  7.2 96.6 %copy-start.3 = (s32[1,8]{1,0:T(1,128)S(1)}, s32[1,8]{1,0:T(1,128)}, u32[]{:S(2)}) copy-start(s32[1,8]{1,0:T(1,128)} %param.13) | copy-start | bytes 100
  7.2 96.6 %copy-start.2 = (bf16[4096]{0:T(1024)(128)(2,1)S(1)}, bf16[4096]{0:T(1024)(128)(2,1)}, u32[]{:S(2)}) copy-start(bf16[4096]{0:T(1024)(128)(2,1)} %param.10) | copy-start | bytes 24580
  7.2 96.6 %copy-start.4 = (s32[16]{0:T(128)S(1)}, s32[16]{0:T(128)}, u32[]{:S(2)}) copy-start(s32[16]{0:T(128)} %param.12) | copy-start | bytes 196
  7.2 91.8 %all-gather.3.cloned.1.call-start = ((), (), s32[]{:S(2)}) async-start(), calls=%async_computation.4 | async-start | bytes 4259840 | tf_op jit(solution)/shard_map/all_gather | solution.py:25
  7.9 134.4 %all-gather.5.cloned.1.call-start = ((), (), s32[]{:S(2)}) async-start(), calls=%async_computation.6 | async-start | bytes 1179648 | tf_op jit(solution)/shard_map/all_gather | solution.py:58
  11.1 174.7 %copy-start.1 = (bf16[16,4096]{1,0:T(8,128)(2,1)S(1)}, bf16[16,4096]{1,0:T(8,128)(2,1)}, u32[]{:S(2)}) copy-start(bf16[16,4096]{1,0:T(8,128)(2,1)} %param.9) | copy-start | bytes 393220
  11.1 174.7 %reduce-scatter.6.cloned.1.call-start = ((), (), s32[]{:S(2)}) async-start(), calls=%async_computation.5 | async-start | bytes 1179648 | tf_op jit(solution)/shard_map/reduce_scatter | solution.py:28
  192.2 198.1 %all-to-all-start = ((bf16[64,16,4096]{2,1,0:T(8,128)(2,1)}), bf16[64,16,4096]{2,1,0:T(8,128)(2,1)}, u32[]{:S(2)}, u32[]{:S(2)}) async-start(bf16[64,16,4096]{2,1,0:T(8,128)(2,1)} %stack.2), calls=%async_computation.1 | async-start | bytes 16777216 | tf_op jit(solution)/shard_map/all_to_all | solution.py:13
  202.6 81.1 %all-reduce.2.cloned.1.call-start = ((), (), s32[]{:S(2)}) async-start(), calls=%async_computation.7 | async-start | bytes 1048576 | tf_op jit(solution)/shard_map/psum | solution.py:71
  203.8 236.9 %reduce-scatter.10.cloned.1.call-start = ((), (), s32[]{:S(2)}) async-start(), calls=%async_computation.9 | async-start | bytes 2129920
  286.7 198.8 %reduce-scatter.8.cloned.1.call-start = ((), (), s32[]{:S(2)}) async-start(), calls=%async_computation.8 | async-start | bytes 1179648 | tf_op jit(solution)/shard_map/reduce_scatter | solution.py:88
Sparse Core Ops, SparseCore 0:
  11.4 87.5 all-gather.2
  101.6 40.6 all-gather.4
  145.2 40.5 reduce-scatter.5
  205.5 78.2 all-reduce.1
  288.2 152.4 reduce-scatter.9
  443.4 42.0 reduce-scatter.7
